TPU v7x, 256 devices: a whole 4x4x8 slice. The times are simulated.
256 devices in a mesh: section: 4 (over x), seq: 16 (over z, y_lo), dp: 4 (over y_hi, core).
Axes of the slice: x: 4, y: 4 (y_hi: 2, y_lo: 2; y = y_hi * 2 + y_lo), z: 8, core: 2. Of those that a mesh axis runs over, the one named last changes fastest.
Arguments:
- main_hidden: bfloat16 [4, 4, 2048, 7168], P('section', 'dp', 'seq'), may hold values from -6 to 6
- embedded: bfloat16 [4, 4, 2048, 7168], P('section', 'dp', 'seq'), may hold values from -6 to 6
- cotangent: bfloat16 [4, 4, 2048, 7168], P('section', 'dp', 'seq'), may hold values from -6 to 6
- slot_token: int32 [4, 4, 2, 96], P('section', 'dp', None, 'seq'), may hold values from 0 to 127, as said below
- slot_count: int32 [4, 4, 2, 16], P('section', 'dp', None, 'seq'), may hold values from 1 to 6, as said below
- route_gate: float32 [4, 4, 2, 96], P('section', 'dp', None, 'seq'), may hold values from 0.2 to 2
- norm_gain: float32 [2, 2, 7168], replicated, may hold values from 0.5 to 1.5
- expert_weight: bfloat16 [2, 3, 7168, 2048], P(None, None, 'seq', 'dp'), may hold values from -0.0625 to 0.0625
Outputs:
- hidden_grad: bfloat16 [4, 4, 2048, 7168], P('section', 'dp', 'seq')
- expert_grad: bfloat16 [4, 2, 3, 7168, 2048], P('section', None, None, 'seq', 'dp')
- gain_grad: float32 [4, 2, 2, 7168], P('section', None, None, ('seq', 'dp'))
Inputs may be any that keep to these rules, and one draw needn't show every extreme that they name: `slot_token`: the slots of one device and depth name distinct positions of that device's block. `slot_count`: in every micro-batch, sequence and depth some device has all 6 slots live.
All inputs are finite; a program needn't handle non-finite values.
Results may differ from a plain program's by a relative error of at most 0.0077.
Values may be sent and summed in bfloat16 or wider, within the bound.
A program may use at most 128 MiB of HBM per device.

v0:
```python
import jax
import jax.numpy as jnp
from jax import lax
from jax.sharding import PartitionSpec as P

eps_norm = 1e-06


def from_behind(value, axis, steps):
    count = lax.axis_size(axis)
    pairs = [(source, (source + steps) % count) for source in range(count)]
    return lax.ppermute(value, axis, pairs)


def from_behind_2(array, axis, by):
    size = lax.axis_size(axis)
    pairs = [(i, i + by) for i in range(size) if 0 <= i + by < size]
    return lax.ppermute(array, axis, pairs)


def normed(value):
    wide = value.astype(jnp.float32)
    scale = lax.rsqrt(jnp.mean(wide * wide, axis=-1, keepdims=True) + eps_norm)
    return (wide * scale, scale)


def norm_back(grad, unit, scale):
    inner = jnp.mean(grad * unit, axis=-1, keepdims=True)
    return (grad - unit * inner) * scale


def contract_rows(left, right):
    return lax.dot_general(
        left, right, (((0,), (0,)), ((), ())), preferred_element_type=jnp.float32
    )


def contract_last(left, right):
    return lax.dot_general(
        left, right, (((1,), (1,)), ((), ())), preferred_element_type=jnp.float32
    )


def spread_rows(rows):
    parts = lax.all_to_all(rows, "seq", split_axis=1, concat_axis=0, tiled=True)
    return lax.all_gather(parts, "dp", axis=0, tiled=True)


def return_rows(partial_rows, capacity):
    blocks = partial_rows.reshape(
        lax.axis_size("dp"), lax.axis_size("seq"), capacity, partial_rows.shape[1]
    )
    back = lax.all_to_all(blocks, "seq", split_axis=1, concat_axis=3, tiled=True)
    total = lax.psum_scatter(back, "dp", scatter_dimension=0, tiled=True)
    return total.reshape(capacity, -1)


def pre_grads(d_act, gate_in, up_in):
    sig = jax.nn.sigmoid(gate_in)
    d_gate = (d_act * up_in * sig * (1.0 + gate_in * (1.0 - sig))).astype(jnp.bfloat16)
    d_up = (d_act * jax.nn.silu(gate_in)).astype(jnp.bfloat16)
    return (d_gate, d_up)


def local(
    main_hidden, embedded, cotangent, slot_token, slot_count, route_gate, norm_gain, expert_weight
):
    depths = norm_gain.shape[0]
    tokens_here = main_hidden.shape[2]
    capacity = slot_token.shape[3]
    hidden = from_behind(main_hidden, "section", 1)[0, 0]
    own_rows = embedded[0, 0]
    ahead = from_behind_2(own_rows[:depths], "seq", -1)
    padded = jnp.concatenate([own_rows, ahead], 0)
    places = jnp.arange(capacity, dtype=jnp.int32)
    current = hidden
    saved = []
    for depth in range(depths):
        shifted = padded[depth + 1 : depth + 1 + tokens_here]
        unit_h, scale_h = normed(current)
        unit_e, scale_e = normed(shifted)
        mixed = (unit_h * norm_gain[depth, 0] + unit_e * norm_gain[depth, 1]).astype(jnp.bfloat16)
        tokens = slot_token[0, 0, depth]
        live = places < slot_count[0, 0, depth, 0]
        weight = route_gate[0, 0, depth] * live.astype(jnp.float32)
        rows = mixed[tokens] * live[:, None].astype(jnp.bfloat16)
        quarter = spread_rows(rows)
        gate_part = jnp.dot(quarter, expert_weight[depth, 0], preferred_element_type=jnp.float32)
        up_part = jnp.dot(quarter, expert_weight[depth, 1], preferred_element_type=jnp.float32)
        gate_in, up_in = lax.psum((gate_part, up_part), "seq")
        act = (jax.nn.silu(gate_in) * up_in).astype(jnp.bfloat16)
        result = return_rows(contract_last(act, expert_weight[depth, 2]), capacity)
        current = (
            mixed.astype(jnp.float32).at[tokens].add(result * weight[:, None]).astype(jnp.bfloat16)
        )
        saved.append((unit_h, scale_h, unit_e, tokens, live, weight, quarter, gate_in, up_in, act))
    grad = cotangent[0, 0].astype(jnp.float32)
    weight_grads = [None] * depths
    gain_terms = [None] * depths
    for depth in reversed(range(depths)):
        unit_h, scale_h, unit_e, tokens, live, weight, quarter, gate_in, up_in, act = saved[depth]
        dout = (grad[tokens] * weight[:, None]).astype(jnp.bfloat16)
        dout_quarter = spread_rows(dout)
        act_part = jnp.dot(
            dout_quarter, expert_weight[depth, 2], preferred_element_type=jnp.float32
        )
        down_grad = contract_rows(dout_quarter, act)
        d_act = lax.psum(act_part, "seq")
        d_gate, d_up = pre_grads(d_act, gate_in, up_in)
        gate_grad = contract_rows(quarter, d_gate)
        up_grad = contract_rows(quarter, d_up)
        partial_rows = contract_last(d_gate, expert_weight[depth, 0]) + contract_last(
            d_up, expert_weight[depth, 1]
        )
        d_rows = return_rows(partial_rows, capacity)
        d_mixed = grad.at[tokens].add(d_rows * live[:, None].astype(jnp.float32))
        gain_terms[depth] = jnp.stack([jnp.sum(d_mixed * unit_h, 0), jnp.sum(d_mixed * unit_e, 0)])
        weight_grads[depth] = jnp.stack([gate_grad, up_grad, down_grad])
        grad = norm_back(d_mixed * norm_gain[depth, 0], unit_h, scale_h)
    gain_grad = lax.psum_scatter(
        jnp.stack(gain_terms), ("seq", "dp"), scatter_dimension=2, tiled=True
    )
    hidden_grad = from_behind(grad.astype(jnp.bfloat16)[None, None], "section", -1)
    expert_grad = jnp.stack(weight_grads).astype(jnp.bfloat16)[None]
    return (hidden_grad, expert_grad, gain_grad[None])


def solution(mesh):
    return jax.shard_map(
        local,
        mesh=mesh,
        in_specs=(
            P("section", "dp", "seq", None),
            P("section", "dp", "seq", None),
            P("section", "dp", "seq", None),
            P("section", "dp", None, "seq"),
            P("section", "dp", None, "seq"),
            P("section", "dp", None, "seq"),
            P(),
            P(None, None, "seq", "dp"),
        ),
        out_specs=(
            P("section", "dp", "seq", None),
            P("section", None, None, "seq", "dp"),
            P("section", None, None, ("seq", "dp")),
        ),
        check_vma=False,
    )
```

profile of v0, /device:TPU:2, one launch (start us, length us, event | category | flops | bytes accessed | tf_op | source)
XLA Modules:
  0.0 1106.0 jit_solution(5909491801143368804)
XLA Ops:
  14.8 3.7 fusion.18
  18.5 33.0 %collective-permute-done = bf16[1,1,128,7168]{3,2,1,0:T(8,128)(2,1)S(1)} collective-permute-done((bf16[1,1,128,7168]{3,2,1,0:T(8,128)(2,1)}, bf16[1,1,128,7168]{3,2,1,0:T(8,128)(2,1)S(1)}, u32[]{:S(2)}, u32[]{:S(2)}) %collective-permute-start) | collective-permute-done | bytes 1835040 | tf_op jit(solution)/shard_map/ppermute | solution.py:12
  51.9 3.4 fusion.87
  58.1 19.9 %all_to_all.118 = bf16[6,16,448]{2,0,1:T(8,128)(2,1)S(1)} all-to-all(bf16[6,16,448]{2,0,1:T(8,128)(2,1)S(1)} %copy.77), channel_id=1, replica_groups=mesh['section'=4,'seq'=16,'dp'=4] {'seq'}, dimensions={1} | all-to-all | bytes 172032 | tf_op jit(solution)/shard_map/all_to_all | solution.py:45
  78.1 8.0 all_gather.13
  90.7 138.8 %all-reduce.10.cloned.1.call-done = (f32[384,512]{1,0:T(8,128)}, f32[384,512]{1,0:T(8,128)}) async-done(((f32[384,512]{1,0:T(8,128)}, f32[384,512]{1,0:T(8,128)}), (f32[384,512]{1,0:T(8,128)}, f32[384,512]{1,0:T(8,128)})) %all-reduce.10.cloned.1.call-update) | async-done | bytes 1572880 | tf_op jit(solution)/shard_map/psum | solution.py:90
  233.2 21.8 %all_to_all.119 = f32[4,16,6,448]{3,0,2,1:T(4,128)S(1)} all-to-all(f32[4,16,6,448]{3,0,2,1:T(4,128)S(1)} %copy.79), channel_id=1, replica_groups=mesh['section'=4,'seq'=16,'dp'=4] {'seq'}, dimensions={1} | all-to-all | bytes 1376256 | tf_op jit(solution)/shard_map/all_to_all | solution.py:53
  256.8 3.7 bitcast_convert_fusion
  265.4 3.5 all-to-all-start
  269.6 9.1 all-to-all-done
  278.7 10.3 all_gather.12
  291.7 5.1 scatter_custom_fusion
  306.5 5.0 all-to-all-start.3
  314.1 7.1 all-to-all-done.3
  321.2 7.6 all_gather.14
  333.5 145.2 %all-reduce.8.cloned.1.call-done = (f32[384,512]{1,0:T(8,128)}, f32[384,512]{1,0:T(8,128)}, f32[384,512]{1,0:T(8,128)}) async-done(((f32[384,512]{1,0:T(8,128)}, f32[384,512]{1,0:T(8,128)}, f32[384,512]{1,0:T(8,128)}), (f32[384,512]{1,0:T(8,128)}, f32[384,512]{1,0:T(8,128)}, f32[384,512]{1,0:T(8,128)})) %all-reduce.8.cloned.1.call-update) | async-done | bytes 2359312 | tf_op jit(solution)/shard_map/psum | solution.py:90
  490.9 21.0 %all_to_all.120 = f32[4,16,6,448]{3,0,2,1:T(4,128)S(1)} all-to-all(f32[4,16,6,448]{3,0,2,1:T(4,128)S(1)} %copy.84), channel_id=1, replica_groups=mesh['section'=4,'seq'=16,'dp'=4] {'seq'}, dimensions={1} | all-to-all | bytes 1376256 | tf_op jit(solution)/shard_map/all_to_all | solution.py:53
  516.5 31.8 %reduce-scatter.9.cloned.1.call-done = f32[1,1,6,7168]{3,2,1,0:T(8,128)} async-done(((f32[4,1,6,7168]{3,2,1,0:T(8,128)}), f32[1,1,6,7168]{3,2,1,0:T(8,128)}) %reduce-scatter.9.cloned.1.call-update) | async-done | bytes 172048 | tf_op jit(solution)/shard_map/reduce_scatter | solution.py:54
  548.3 5.1 scatter_custom_fusion.1
  553.3 4.9 fusion.22
  564.0 16.6 %all_to_all.121 = bf16[6,16,448]{2,0,1:T(8,128)(2,1)S(1)} all-to-all(bf16[6,16,448]{2,0,1:T(8,128)(2,1)S(1)} %copy.87), channel_id=1, replica_groups=mesh['section'=4,'seq'=16,'dp'=4] {'seq'}, dimensions={1} | all-to-all | bytes 172032 | tf_op jit(solution)/shard_map/all_to_all | solution.py:45
  580.7 7.6 all_gather.15
  591.3 134.4 %all-reduce.6.cloned.1.call-done = f32[384,512]{1,0:T(8,128)} async-done(((f32[384,512]{1,0:T(8,128)}), f32[384,512]{1,0:T(8,128)}) %all-reduce.6.cloned.1.call-update) | async-done | bytes 786448 | tf_op jit(solution)/shard_map/psum | solution.py:108
  738.8 5.8 all-to-all-start.6
  751.5 9.0 all-to-all-done.6
  771.2 27.7 %reduce-scatter.11.cloned.1.call-done = f32[1,1,6,7168]{3,2,1,0:T(8,128)} async-done(((f32[4,1,6,7168]{3,2,1,0:T(8,128)}), f32[1,1,6,7168]{3,2,1,0:T(8,128)}) %reduce-scatter.11.cloned.1.call-update) | async-done | bytes 172048 | tf_op jit(solution)/shard_map/reduce_scatter | solution.py:54
  798.9 5.1 scatter_custom_fusion.2
  804.0 4.3 fusion.29
  811.2 6.8 copy.96
  818.0 7.9 reshape.298
  829.3 265.3 %reduce-scatter.13.cloned.1.call-done = f32[112,4]{1,0:T(8,128)} async-done(((f32[7168,4]{1,0:T(8,128)}), f32[112,4]{1,0:T(8,128)}) %reduce-scatter.13.cloned.1.call-update) | async-done | bytes 1808
  1096.3 2.8 copy.113
  (157 shorter events, 109.8 us)
Async XLA Ops:
  7.2 222.3 %all-reduce.10.cloned.1.call-start = ((), (), s32[]{:S(2)}) async-start(), calls=%async_computation.17 | async-start | bytes 3145728 | tf_op jit(solution)/shard_map/psum | solution.py:90
  8.1 6.6 collective-permute-start.1
  9.4 42.0 %collective-permute-start = (bf16[1,1,128,7168]{3,2,1,0:T(8,128)(2,1)}, bf16[1,1,128,7168]{3,2,1,0:T(8,128)(2,1)S(1)}, u32[]{:S(2)}, u32[]{:S(2)}) collective-permute-start(bf16[1,1,128,7168]{3,2,1,0:T(8,128)(2,1)} %param.8), channel_id=1, source_target_pairs={{0,64},{64,128},{128,192},{192,0},{1,65},{65,129},{129,193},{193,1... | collective-permute-start | bytes 5505032 | tf_op jit(solution)/shard_map/ppermute | solution.py:12
  11.8 279.9 %copy-start.25 = (s32[6]{0:T(128)}, s32[6]{0:T(128)S(1)}, u32[]{:S(2)}) copy-start(s32[6]{0:T(128)S(1)} %get-tuple-element.32) | copy-start | bytes 76
  13.1 42.3 %copy-start.18 = (s32[1024]{0:T(1024)}, s32[1024]{0:T(1024)S(1)}, u32[]{:S(2)}) copy-start(s32[1024]{0:T(1024)S(1)} %pad_clamp_fusion) | copy-start | bytes 12292
  18.4 36.9 %copy-start.5 = (bf16[128,7168]{1,0:T(8,128)(2,1)}, bf16[128,7168]{1,0:T(8,128)(2,1)S(1)}, u32[]{:S(2)}) copy-start(bf16[128,7168]{1,0:T(8,128)(2,1)S(1)} %get-tuple-element.19) | copy-start | bytes 5505028
  18.4 36.9 %copy-start.23 = (f32[128]{0:T(128)}, f32[128]{0:T(128)S(1)}, u32[]{:S(2)}) copy-start(f32[128]{0:T(128)S(1)} %add_rsqrt_fusion.2) | copy-start | bytes 1540
  90.7 201.0 %reduce-scatter.7.cloned.1.call-start = ((), (), s32[]{:S(2)}) async-start(), calls=%async_computation.11 | async-start | bytes 1146880 | tf_op jit(solution)/shard_map/reduce_scatter | solution.py:54
  231.1 25.6 %copy-start.7 = (bf16[384,512]{1,0:T(8,128)(2,1)}, bf16[384,512]{1,0:T(8,128)(2,1)S(1)}, u32[]{:S(2)}) copy-start(bf16[384,512]{1,0:T(8,128)(2,1)S(1)} %multiply_convert_fusion.5) | copy-start | bytes 1179652
  256.7 6.5 copy-start.26
  264.6 34.9 %copy-start.21 = (f32[6]{0:T(128)}, f32[6]{0:T(128)S(1)}, u32[]{:S(2)}) copy-start(f32[6]{0:T(128)S(1)} %get-tuple-element.30) | copy-start | bytes 76
  265.4 13.2 %all-to-all-start = ((bf16[6,16,448]{2,0,1:T(8,128)(2,1)}), bf16[6,16,448]{2,0,1:T(8,128)(2,1)S(1)}, u32[]{:S(2)}, u32[]{:S(2)}) async-start(bf16[6,16,448]{2,0,1:T(8,128)(2,1)} %copy.76), calls=%async_computation | async-start | bytes 262144 | tf_op jit(solution)/shard_map/all_to_all | solution.py:45
  289.0 22.8 %copy-start.16 = (bf16[384,448]{1,0:T(8,128)(2,1)}, bf16[384,448]{1,0:T(8,128)(2,1)S(1)}, u32[]{:S(2)}) copy-start(bf16[384,448]{1,0:T(8,128)(2,1)S(1)} %all_gather.12) | copy-start | bytes 1032196
  296.8 3.9 copy-start.4
  306.5 14.7 %all-to-all-start.3 = ((bf16[6,16,448]{2,0,1:T(8,128)(2,1)}), bf16[6,16,448]{2,0,1:T(8,128)(2,1)S(1)}, u32[]{:S(2)}, u32[]{:S(2)}) async-start(bf16[6,16,448]{2,0,1:T(8,128)(2,1)} %copy.82), calls=%async_computation.4 | async-start | bytes 262144 | tf_op jit(solution)/shard_map/all_to_all | solution.py:45
  311.6 167.1 %all-reduce.8.cloned.1.call-start = ((), (), s32[]{:S(2)}) async-start(), calls=%async_computation.16 | async-start | bytes 4718592 | tf_op jit(solution)/shard_map/psum | solution.py:90
  333.4 214.8 %reduce-scatter.9.cloned.1.call-start = ((), (), s32[]{:S(2)}) async-start(), calls=%async_computation.12 | async-start | bytes 1146880 | tf_op jit(solution)/shard_map/reduce_scatter | solution.py:54
  515.8 210.0 %all-reduce.6.cloned.1.call-start = ((), (), s32[]{:S(2)}) async-start(), calls=%async_computation.13 | async-start | bytes 1572864 | tf_op jit(solution)/shard_map/psum | solution.py:108
  553.3 4.9 copy-start.1
  553.3 5.0 copy-start.3
  558.3 5.6 copy-start.22
  738.8 21.6 %all-to-all-start.6 = ((f32[4,16,6,448]{3,0,2,1:T(4,128)}), f32[4,16,6,448]{3,0,2,1:T(4,128)}, u32[]{:S(2)}, u32[]{:S(2)}) async-start(f32[4,16,6,448]{3,0,2,1:T(4,128)} %copy.89), calls=%async_computation.8 | async-start | bytes 1572864 | tf_op jit(solution)/shard_map/all_to_all | solution.py:53
  744.6 54.4 %reduce-scatter.11.cloned.1.call-start = ((), (), s32[]{:S(2)}) async-start(), calls=%async_computation.14 | async-start | bytes 1146880 | tf_op jit(solution)/shard_map/reduce_scatter | solution.py:54
  751.5 16.7 %copy-start.17 = (f32[7168]{0:T(1024)S(1)}, f32[7168]{0:T(1024)}, u32[]{:S(2)}) copy-start(f32[7168]{0:T(1024)} %get-tuple-element.8) | copy-start | bytes 86020
  751.5 16.8 %copy-start.8 = (bf16[384,512]{1,0:T(8,128)(2,1)S(1)}, bf16[384,512]{1,0:T(8,128)(2,1)}, u32[]{:S(2)}) copy-start(bf16[384,512]{1,0:T(8,128)(2,1)} %copy-done.7) | copy-start | bytes 1179652
  751.5 16.8 %copy-start.11 = (bf16[384,448]{1,0:T(8,128)(2,1)S(1)}, bf16[384,448]{1,0:T(8,128)(2,1)}, u32[]{:S(2)}) copy-start(bf16[384,448]{1,0:T(8,128)(2,1)} %copy-done.10) | copy-start | bytes 1032196
  765.4 329.3 %reduce-scatter.13.cloned.1.call-start = ((), (), s32[]{:S(2)}) async-start(), calls=%async_computation.15 | async-start | bytes 3727360
  765.6 3.9 copy-start.13
  768.3 35.7 %copy-start.20 = (f32[128]{0:T(128)S(1)}, f32[128]{0:T(128)}, u32[]{:S(2)}) copy-start(f32[128]{0:T(128)} %copy-done.19) | copy-start | bytes 1540
  768.3 35.7 %copy-start.24 = (f32[128]{0:T(128)S(1)}, f32[128]{0:T(128)}, u32[]{:S(2)}) copy-start(f32[128]{0:T(128)} %copy-done.23) | copy-start | bytes 1540
  804.0 4.4 copy-start
  810.5 285.8 %collective-permute-start.2 = (bf16[1,1,128,7168]{3,2,1,0:T(8,128)(2,1)}, bf16[1,1,128,7168]{3,2,1,0:T(8,128)(2,1)}, u32[]{:S(2)}, u32[]{:S(2)}) collective-permute-start(bf16[1,1,128,7168]{3,2,1,0:T(8,128)(2,1)} %fusion.32), channel_id=1, source_target_pairs={{0,192},{64,0},{128,64},{192,128},{1,193},{65,1},{129,65},{193,129... | collective-permute-start | bytes 5505032 | tf_op jit(solution)/shard_map/ppermute | solution.py:12
  (8 other events, 12.4 us)
Sparse Core Ops, SparseCore 0:
  90.8 138.6 all-reduce.9
  256.9 34.7 reduce-scatter.6
  333.6 145.0 all-reduce.7
  515.9 32.3 reduce-scatter.8
  591.5 134.2 all-reduce.5
  765.5 33.4 reduce-scatter.10
  826.1 268.5 reduce-scatter.12
where the time goes:
time: 1110 us
  waiting for transfers between devices  804 us (72%)
  blocking collectives  113 us (10%)
  local copies, waits for them, and re-layouts  63.1 us (6%)
  other arithmetic  60.9 us (5%)
  matrix products  31.8 us (3%)
  starting transfers between devices  18.4 us (2%)
  between operations  14.6 us (1%)
    psum x2, waiting for transfers between devices, local(): gate_in, up_in = lax.psum((gate_part, up_part), 'seq')  284 us
    unnamed x8, waiting for transfers between devices  265 us
    psum x1, waiting for transfers between devices, local(): d_act = lax.psum(act_part, 'seq')  134 us
    reduce_scatter x3, waiting for transfers between devices, return_rows(): total = lax.psum_scatter(back, 'dp', scatter_dimension=0, tiled=True)  62.3 us
    all_to_all x2, blocking collectives, return_rows(): lax.all_to_all(blocks, 'seq', split_axis=1, concat_axis=3, tiled=True)  42.8 us
    all_to_all x2, blocking collectives, spread_rows(): parts = lax.all_to_all(rows, 'seq', split_axis=1, concat_axis=0, tiled=True)  36.5 us
    all_gather x4, blocking collectives, spread_rows(): return lax.all_gather(parts, 'dp', axis=0, tiled=True)  33.6 us
    ppermute x2, waiting for transfers between devices, from_behind(): return lax.ppermute(value, axis, pairs)  33 us
  transfers between devices with their start and end apart: 13, of which 11 were waited for; matrix products, arithmetic and copies ran while one was open for 5% of the time, Pallas kernels for 0%

commit v1 on v0

--- a/solution.py
+++ b/solution.py
@@ -105,7 +105,7 @@
             dout_quarter, expert_weight[depth, 2], preferred_element_type=jnp.float32
         )
         down_grad = contract_rows(dout_quarter, act)
-        d_act = lax.psum(act_part, "seq")
+        d_act = jnp.sum(jax.lax.all_gather(act_part, "seq"), axis=0)
         d_gate, d_up = pre_grads(d_act, gate_in, up_in)
         gate_grad = contract_rows(quarter, d_gate)
         up_grad = contract_rows(quarter, d_up)

time: 1110 us -> 1490 us (1.34)
  waiting for transfers between devices: 804 us -> 1140 us
  blocking collectives: 113 us -> 146 us
    all_gather x0 -> x2, waiting for transfers between devices: none -> 486 us  [local(): d_act = jnp.sum(jax.lax.all_gather(act_part, 'seq'), axis=0)]
    psum x1 -> x0, waiting for transfers between devices: 134 us -> none  [local(): d_act = lax.psum(act_part, 'seq')]
    all_to_all x2 -> x4, blocking collectives: 36.5 us -> 64.8 us  [spread_rows(): parts = lax.all_to_all(rows, 'seq', split_axis=1, concat_axis=0, tiled=True)]
    all_to_all x2 -> x0, waiting for transfers between devices: 16.2 us -> none  [spread_rows(): parts = lax.all_to_all(rows, 'seq', split_axis=1, concat_axis=0, tiled=True)]
    unnamed x8 -> x9, waiting for transfers between devices: 265 us -> 266 us
  transfers between devices with their start and end apart: 13 -> 12, of which waited for: 11 -> 10; matrix products, arithmetic and copies ran while one was open for 5% -> 5% of each run, Pallas kernels for 0% -> 0%
where the time goes in v1:
time: 1490 us; the launch traced here: 1480 us
  waiting for transfers between devices  1140 us (77%)
  blocking collectives  146 us (10%)
  other arithmetic  74.7 us (5%)
  local copies, waits for them, and re-layouts  62.8 us (4%)
  matrix products  30.9 us (2%)
    all_gather x2, waiting for transfers between devices, local(): d_act = jnp.sum(jax.lax.all_gather(act_part, 'seq'), axis=0)  486 us
    psum x2, waiting for transfers between devices, local(): gate_in, up_in = lax.psum((gate_part, up_part), 'seq')  281 us
    unnamed x9, waiting for transfers between devices  266 us
    all_to_all x4, blocking collectives, spread_rows(): parts = lax.all_to_all(rows, 'seq', split_axis=1, concat_axis=0, tiled=True)  64.8 us
    reduce_scatter x3, waiting for transfers between devices, return_rows(): total = lax.psum_scatter(back, 'dp', scatter_dimension=0, tiled=True)  59.7 us
    all_to_all x2, blocking collectives, return_rows(): lax.all_to_all(blocks, 'seq', split_axis=1, concat_axis=3, tiled=True)  43.6 us
    all_gather x4, blocking collectives, spread_rows(): return lax.all_gather(parts, 'dp', axis=0, tiled=True)  37.4 us
    ppermute x2, waiting for transfers between devices, from_behind(): return lax.ppermute(value, axis, pairs)  33.1 us
  transfers between devices with their start and end apart: 12, of which 10 were waited for; matrix products, arithmetic and copies ran while one was open for 5% of the time, Pallas kernels for 0%

profile of v1, /device:TPU:2, one launch (start us, length us, event | category | flops | bytes accessed | tf_op | source)
XLA Modules:
  0.0 1483.3 jit_solution(1301371497363858820)
XLA Ops:
  14.7 3.7 fusion.18
  18.4 33.1 %collective-permute-done = bf16[1,1,128,7168]{3,2,1,0:T(8,128)(2,1)S(1)} collective-permute-done((bf16[1,1,128,7168]{3,2,1,0:T(8,128)(2,1)}, bf16[1,1,128,7168]{3,2,1,0:T(8,128)(2,1)S(1)}, u32[]{:S(2)}, u32[]{:S(2)}) %collective-permute-start) | collective-permute-done | bytes 1835040 | tf_op jit(solution)/shard_map/ppermute | solution.py:12
  51.9 3.4 fusion.87
  58.1 19.9 %all_to_all.118 = bf16[6,16,448]{2,0,1:T(8,128)(2,1)S(1)} all-to-all(bf16[6,16,448]{2,0,1:T(8,128)(2,1)S(1)} %copy.77), channel_id=1, replica_groups=mesh['section'=4,'seq'=16,'dp'=4] {'seq'}, dimensions={1} | all-to-all | bytes 172032 | tf_op jit(solution)/shard_map/all_to_all | solution.py:45
  78.1 8.0 all_gather.27
  90.7 138.8 %all-reduce.7.cloned.1.call-done = (f32[384,512]{1,0:T(8,128)}, f32[384,512]{1,0:T(8,128)}) async-done(((f32[384,512]{1,0:T(8,128)}, f32[384,512]{1,0:T(8,128)}), (f32[384,512]{1,0:T(8,128)}, f32[384,512]{1,0:T(8,128)})) %all-reduce.7.cloned.1.call-update) | async-done | bytes 1572880 | tf_op jit(solution)/shard_map/psum | solution.py:90
  233.2 21.8 %all_to_all.119 = f32[4,16,6,448]{3,0,2,1:T(4,128)S(1)} all-to-all(f32[4,16,6,448]{3,0,2,1:T(4,128)S(1)} %copy.79), channel_id=1, replica_groups=mesh['section'=4,'seq'=16,'dp'=4] {'seq'}, dimensions={1} | all-to-all | bytes 1376256 | tf_op jit(solution)/shard_map/all_to_all | solution.py:53
  256.8 3.7 bitcast_convert_fusion
  264.7 12.3 all_to_all.120
  277.1 9.1 all_gather.24
  290.2 5.0 scatter_custom_fusion
  304.5 16.0 %all_to_all.121 = bf16[6,16,448]{2,0,1:T(8,128)(2,1)S(1)} all-to-all(bf16[6,16,448]{2,0,1:T(8,128)(2,1)S(1)} %copy.82), channel_id=1, replica_groups=mesh['section'=4,'seq'=16,'dp'=4] {'seq'}, dimensions={1} | all-to-all | bytes 172032 | tf_op jit(solution)/shard_map/all_to_all | solution.py:45
  320.5 12.3 all_gather.28
  337.5 223.5 %all-gather.5.cloned.1.call-done = f32[6144,512]{1,0:T(8,128)} async-done(((f32[384,512]{1,0:T(8,128)}), f32[6144,512]{1,0:T(8,128)}) %all-gather.5.cloned.1.call-update) | async-done | bytes 12582928 | tf_op jit(solution)/shard_map/all_gather | solution.py:108
  561.0 7.0 reduce_sum.108
  568.1 142.5 %all-reduce.5.cloned.1.call-done = (f32[384,512]{1,0:T(8,128)}, f32[384,512]{1,0:T(8,128)}) async-done(((f32[384,512]{1,0:T(8,128)}, f32[384,512]{1,0:T(8,128)}), (f32[384,512]{1,0:T(8,128)}, f32[384,512]{1,0:T(8,128)})) %all-reduce.5.cloned.1.call-update) | async-done | bytes 1572880 | tf_op jit(solution)/shard_map/psum | solution.py:90
  722.9 21.8 %all_to_all.122 = f32[4,16,6,448]{3,0,2,1:T(4,128)S(1)} all-to-all(f32[4,16,6,448]{3,0,2,1:T(4,128)S(1)} %copy.84), channel_id=1, replica_groups=mesh['section'=4,'seq'=16,'dp'=4] {'seq'}, dimensions={1} | all-to-all | bytes 1376256 | tf_op jit(solution)/shard_map/all_to_all | solution.py:53
  749.2 32.1 %reduce-scatter.9.cloned.1.call-done = f32[1,1,6,7168]{3,2,1,0:T(8,128)} async-done(((f32[4,1,6,7168]{3,2,1,0:T(8,128)}), f32[1,1,6,7168]{3,2,1,0:T(8,128)}) %reduce-scatter.9.cloned.1.call-update) | async-done | bytes 172048 | tf_op jit(solution)/shard_map/reduce_scatter | solution.py:54
  781.4 5.1 scatter_custom_fusion.1
  786.4 5.0 fusion.22
  797.1 16.6 %all_to_all.123 = bf16[6,16,448]{2,0,1:T(8,128)(2,1)S(1)} all-to-all(bf16[6,16,448]{2,0,1:T(8,128)(2,1)S(1)} %copy.87), channel_id=1, replica_groups=mesh['section'=4,'seq'=16,'dp'=4] {'seq'}, dimensions={1} | all-to-all | bytes 172032 | tf_op jit(solution)/shard_map/all_to_all | solution.py:45
  813.7 7.9 all_gather.29
  824.6 262.2 %all-gather.7.cloned.1.call-done = f32[6144,512]{1,0:T(8,128)} async-done(((f32[384,512]{1,0:T(8,128)}), f32[6144,512]{1,0:T(8,128)}) %all-gather.7.cloned.1.call-update) | async-done | bytes 12582928 | tf_op jit(solution)/shard_map/all_gather | solution.py:108
  1086.9 7.0 reduce_sum.114
  1107.0 8.4 all-to-all-start.6
  1121.3 17.0 %all-to-all-done.6 = f32[4,16,6,448]{3,0,2,1:T(4,128)} async-done(((f32[4,16,6,448]{3,0,2,1:T(4,128)}), f32[4,16,6,448]{3,0,2,1:T(4,128)}, u32[]{:S(2)}, u32[]{:S(2)}) %all-to-all-start.6) | async-done | bytes 688160 | tf_op jit(solution)/shard_map/all_to_all | solution.py:53
  1148.8 27.3 %reduce-scatter.11.cloned.1.call-done = f32[1,1,6,7168]{3,2,1,0:T(8,128)} async-done(((f32[4,1,6,7168]{3,2,1,0:T(8,128)}), f32[1,1,6,7168]{3,2,1,0:T(8,128)}) %reduce-scatter.11.cloned.1.call-update) | async-done | bytes 172048 | tf_op jit(solution)/shard_map/reduce_scatter | solution.py:54
  1176.1 5.0 scatter_custom_fusion.2
  1181.2 4.3 fusion.29
  1188.3 6.9 copy.96
  1195.2 7.9 reshape.300
  1206.5 265.5 %reduce-scatter.13.cloned.1.call-done = f32[112,4]{1,0:T(8,128)} async-done(((f32[7168,4]{1,0:T(8,128)}), f32[112,4]{1,0:T(8,128)}) %reduce-scatter.13.cloned.1.call-update) | async-done | bytes 1808
  (162 shorter events, 108.5 us)
Async XLA Ops:
  7.2 222.3 %all-reduce.7.cloned.1.call-start = ((), (), s32[]{:S(2)}) async-start(), calls=%async_computation.18 | async-start | bytes 3145728 | tf_op jit(solution)/shard_map/psum | solution.py:90
  8.1 6.5 collective-permute-start.1
  9.4 42.0 %collective-permute-start = (bf16[1,1,128,7168]{3,2,1,0:T(8,128)(2,1)}, bf16[1,1,128,7168]{3,2,1,0:T(8,128)(2,1)S(1)}, u32[]{:S(2)}, u32[]{:S(2)}) collective-permute-start(bf16[1,1,128,7168]{3,2,1,0:T(8,128)(2,1)} %param.8), channel_id=1, source_target_pairs={{0,64},{64,128},{128,192},{192,0},{1,65},{65,129},{129,193},{193,1... | collective-permute-start | bytes 5505032 | tf_op jit(solution)/shard_map/ppermute | solution.py:12
  11.8 278.5 %copy-start.26 = (s32[6]{0:T(128)}, s32[6]{0:T(128)S(1)}, u32[]{:S(2)}) copy-start(s32[6]{0:T(128)S(1)} %get-tuple-element.31) | copy-start | bytes 76
  13.1 42.3 %copy-start.19 = (s32[1024]{0:T(1024)}, s32[1024]{0:T(1024)S(1)}, u32[]{:S(2)}) copy-start(s32[1024]{0:T(1024)S(1)} %pad_clamp_fusion) | copy-start | bytes 12292
  18.3 37.0 %copy-start.5 = (bf16[128,7168]{1,0:T(8,128)(2,1)}, bf16[128,7168]{1,0:T(8,128)(2,1)S(1)}, u32[]{:S(2)}) copy-start(bf16[128,7168]{1,0:T(8,128)(2,1)S(1)} %get-tuple-element.18) | copy-start | bytes 5505028
  18.4 37.0 %copy-start.24 = (f32[128]{0:T(128)}, f32[128]{0:T(128)S(1)}, u32[]{:S(2)}) copy-start(f32[128]{0:T(128)S(1)} %add_rsqrt_fusion.2) | copy-start | bytes 1540
  51.9 3.5 copy-start.20
  90.7 199.6 %reduce-scatter.7.cloned.1.call-start = ((), (), s32[]{:S(2)}) async-start(), calls=%async_computation.11 | async-start | bytes 1146880 | tf_op jit(solution)/shard_map/reduce_scatter | solution.py:54
  231.1 25.6 %copy-start.7 = (bf16[384,512]{1,0:T(8,128)(2,1)}, bf16[384,512]{1,0:T(8,128)(2,1)S(1)}, u32[]{:S(2)}) copy-start(bf16[384,512]{1,0:T(8,128)(2,1)S(1)} %multiply_convert_fusion.5) | copy-start | bytes 1179652
  256.7 6.6 copy-start.27
  256.8 304.3 %all-gather.5.cloned.1.call-start = ((), (), s32[]{:S(2)}) async-start(), calls=%async_computation.14 | async-start | bytes 13369344 | tf_op jit(solution)/shard_map/all_gather | solution.py:108
  264.5 30.7 %copy-start.22 = (f32[6]{0:T(128)}, f32[6]{0:T(128)S(1)}, u32[]{:S(2)}) copy-start(f32[6]{0:T(128)S(1)} %get-tuple-element.29) | copy-start | bytes 76
  289.3 421.3 %all-reduce.5.cloned.1.call-start = ((), (), s32[]{:S(2)}) async-start(), calls=%async_computation.17 | async-start | bytes 3145728 | tf_op jit(solution)/shard_map/psum | solution.py:90
  295.3 3.9 copy-start.4
  337.5 443.9 %reduce-scatter.9.cloned.1.call-start = ((), (), s32[]{:S(2)}) async-start(), calls=%async_computation.12 | async-start | bytes 1146880 | tf_op jit(solution)/shard_map/reduce_scatter | solution.py:54
  748.5 338.3 %all-gather.7.cloned.1.call-start = ((), (), s32[]{:S(2)}) async-start(), calls=%async_computation.15 | async-start | bytes 13369344 | tf_op jit(solution)/shard_map/all_gather | solution.py:108
  786.4 5.0 copy-start.1
  786.4 5.0 copy-start.3
  791.4 5.5 copy-start.23
  1107.0 31.3 %all-to-all-start.6 = ((f32[4,16,6,448]{3,0,2,1:T(4,128)}), f32[4,16,6,448]{3,0,2,1:T(4,128)}, u32[]{:S(2)}, u32[]{:S(2)}) async-start(f32[4,16,6,448]{3,0,2,1:T(4,128)} %copy.89), calls=%async_computation.8 | async-start | bytes 1572864 | tf_op jit(solution)/shard_map/all_to_all | solution.py:53
  1115.4 60.7 %reduce-scatter.11.cloned.1.call-start = ((), (), s32[]{:S(2)}) async-start(), calls=%async_computation.13 | async-start | bytes 1146880 | tf_op jit(solution)/shard_map/reduce_scatter | solution.py:54
  1115.4 3.4 copy-start.10
  1121.3 24.6 %copy-start.18 = (f32[7168]{0:T(1024)S(1)}, f32[7168]{0:T(1024)}, u32[]{:S(2)}) copy-start(f32[7168]{0:T(1024)} %get-tuple-element.8) | copy-start | bytes 86020
  1121.3 24.7 %copy-start.8 = (bf16[384,512]{1,0:T(8,128)(2,1)S(1)}, bf16[384,512]{1,0:T(8,128)(2,1)}, u32[]{:S(2)}) copy-start(bf16[384,512]{1,0:T(8,128)(2,1)} %copy-done.7) | copy-start | bytes 1179652
  1121.3 24.7 %copy-start.12 = (bf16[384,448]{1,0:T(8,128)(2,1)S(1)}, bf16[384,448]{1,0:T(8,128)(2,1)}, u32[]{:S(2)}) copy-start(bf16[384,448]{1,0:T(8,128)(2,1)} %copy-done.11) | copy-start | bytes 1032196
  1143.2 328.8 %reduce-scatter.13.cloned.1.call-start = ((), (), s32[]{:S(2)}) async-start(), calls=%async_computation.16 | async-start | bytes 3727360
  1143.3 3.9 copy-start.14
  1146.0 35.2 %copy-start.21 = (f32[128]{0:T(128)S(1)}, f32[128]{0:T(128)}, u32[]{:S(2)}) copy-start(f32[128]{0:T(128)} %copy-done.20) | copy-start | bytes 1540
  1146.0 35.2 %copy-start.25 = (f32[128]{0:T(128)S(1)}, f32[128]{0:T(128)}, u32[]{:S(2)}) copy-start(f32[128]{0:T(128)} %copy-done.24) | copy-start | bytes 1540
  1181.2 4.4 copy-start
  1187.7 286.0 %collective-permute-start.2 = (bf16[1,1,128,7168]{3,2,1,0:T(8,128)(2,1)}, bf16[1,1,128,7168]{3,2,1,0:T(8,128)(2,1)}, u32[]{:S(2)}, u32[]{:S(2)}) collective-permute-start(bf16[1,1,128,7168]{3,2,1,0:T(8,128)(2,1)} %fusion.32), channel_id=1, source_target_pairs={{0,192},{64,0},{128,64},{192,128},{1,193},{65,1},{129,65},{193,129... | collective-permute-start | bytes 5505032 | tf_op jit(solution)/shard_map/ppermute | solution.py:12
  (8 other events, 9.7 us)
Sparse Core Ops, SparseCore 0:
  90.8 138.6 all-reduce.6
  256.9 33.3 reduce-scatter.6
  292.0 268.9 all-gather.4
  563.6 146.9 all-reduce.4
  748.6 32.6 reduce-scatter.8
  824.8 262.0 all-gather.6
  1143.4 32.6 reduce-scatter.10
  1203.3 268.6 reduce-scatter.12
